TPU v7x, 32 devices: a whole 2x2x4 slice. The times are simulated.
32 devices in a mesh: member: 4 (over y, x), slab: 8 (over z, core).
Axes of the slice: x: 2, y: 2, z: 4, core: 2. Of those that a mesh axis runs over, the one named last changes fastest.
Arguments:
- control: float32 [16, 2, 1024, 2048], P('member', None, 'slab'), may hold values from -6 to 6
- perturbation: bfloat16 [16, 2, 1024, 2048], P('member', None, 'slab'), may hold values from -6 to 6
- loc_row: float32 [2, 1024], P(None, 'slab'), may hold values from 0.2 to 2
- loc_col: float32 [2, 2048], replicated, may hold values from 0.2 to 2
- obs_tile: int32 [2048], P('slab'), may hold values from 0 to 4095, as said below
- obs_count: int32 [2048], P('slab'), may hold values from 1 to 128
- obs_value: float32 [2048, 128], P('slab'), may hold values from -12 to 12
Outputs:
- gradient: float32 [16, 2, 1024, 2048], P('member', None, 'slab')
Inputs may be any that keep to these rules, and one draw needn't show every extreme that they name: `obs_tile`: entry i names a tile of slab block i // 256 in that block's numbering, whose columns lie in column share k = (i mod 256) // (256 / 8), i.e. columns k * 2048 / 8 onward; tiles may repeat. cells 0 to obs_count - 1 of a tile are observed.
All inputs are finite; a program needn't handle non-finite values.
Results may differ from a plain program's by a relative error of at most 0.012.
Values may be sent and summed in bfloat16 or wider, within the bound.
A program may use at most 64 MiB of HBM per device.

v0:
```python
import jax
import jax.numpy as jnp
from jax import lax
from jax.sharding import PartitionSpec as P

TILE = 128


def hartley(order):
    index = jnp.arange(order, dtype=jnp.int32)
    product = index[:, None] * index[None, :] % order
    angle = 2.0 * jnp.pi * product.astype(jnp.float32) / order
    table = (jnp.cos(angle) + jnp.sin(angle)) / jnp.sqrt(jnp.float32(order))
    return table.astype(jnp.bfloat16)


def shards(control, perturbation, loc_row, loc_col, obs_tile, obs_count, obs_value):
    members, levels, rows, width = control.shape
    slabs = lax.axis_size("slab")
    height = rows * slabs
    share = width // slabs
    table_y = hartley(height)
    table_x = hartley(width)
    amplitude = loc_row[:, :, None] * loc_col[:, None, :]

    def columns_pass(block):
        product = jnp.einsum("ya,mlac->mlyc", table_y, block, preferred_element_type=jnp.float32)
        return product.astype(jnp.bfloat16)

    scaled = (control * amplitude[None]).astype(jnp.bfloat16)
    along = jnp.dot(scaled.reshape(-1, width), table_x, preferred_element_type=jnp.float32)
    along = along.astype(jnp.bfloat16).reshape(members, levels, rows, width)
    field_cols = columns_pass(
        lax.all_to_all(along, "slab", split_axis=3, concat_axis=2, tiled=True)
    )
    tile_total = levels * rows * (width // TILE)
    all_tiles = lax.all_gather(obs_tile, "slab", axis=0, tiled=True)
    per_peer = obs_tile.shape[0] // slabs
    mine = lax.axis_index("slab")
    listed = lax.dynamic_slice_in_dim(all_tiles.reshape(slabs, slabs, per_peer), mine, 1, 1)
    listed = listed.reshape(slabs, per_peer)
    per_row = width // TILE
    level = listed // (rows * per_row)
    row_in = listed // per_row % rows
    local_tile = listed % per_row - mine * (share // TILE)
    source = jnp.arange(slabs, dtype=jnp.int32)[:, None]
    flat_index = ((level * height + source * rows + row_in) * (share // TILE) + local_tile).reshape(
        -1
    )
    picked = field_cols.reshape(members, -1, TILE)[:, flat_index]
    field_obs = lax.all_to_all(picked, "slab", split_axis=1, concat_axis=1, tiled=True)
    pert_obs = perturbation.reshape(members, -1, TILE)[:, obs_tile].astype(jnp.float32)
    partial_obs = jnp.sum(pert_obs * field_obs.astype(jnp.float32), axis=0)
    cells = lax.psum(partial_obs, "member")
    resid = cells - obs_value
    observed = jnp.arange(TILE, dtype=jnp.int32)[None, :] < obs_count[:, None]
    score = jnp.where(observed, resid / jnp.sqrt(1.0 + resid * resid / 4.0), 0.0)
    adjoint_tiles = jnp.zeros((tile_total, TILE), jnp.float32).at[obs_tile].add(score)
    weighted_obs = (pert_obs * adjoint_tiles[obs_tile][None]).astype(jnp.bfloat16)
    arrived = lax.all_to_all(weighted_obs, "slab", split_axis=1, concat_axis=1, tiled=True)
    empty = jnp.zeros((members, levels * height * (share // TILE), TILE), jnp.bfloat16)
    filled = empty.at[:, flat_index].set(arrived)
    back_cols = columns_pass(filled.reshape(members, levels, height, share))
    back = lax.all_to_all(back_cols, "slab", split_axis=2, concat_axis=3, tiled=True)
    result = jnp.dot(back.reshape(-1, width), table_x, preferred_element_type=jnp.float32)
    return result.reshape(members, levels, rows, width) * amplitude[None]


def solution(mesh):
    placed = (
        P("member", None, "slab", None),
        P("member", None, "slab", None),
        P(None, "slab"),
        P(),
        P("slab"),
        P("slab"),
        P("slab", None),
    )
    return jax.shard_map(
        shards,
        mesh=mesh,
        in_specs=placed,
        out_specs=P("member", None, "slab", None),
        check_vma=False,
    )
```

profile of v0, /device:TPU:0, one launch (start us, length us, event | category | flops | bytes accessed | tf_op | source)
XLA Modules:
  0.0 563.9 jit_solution(10304791134085167966)
XLA Ops:
  6.5 0.0 copy-start.2
  6.5 0.0 copy-start.5
  6.5 0.0 copy-start
  6.5 68.2 %multiply_convert_fusion.9 = bf16[2048,2048]{1,0:T(8,128)(2,1)} fusion(), kind=kLoop, calls=%fused_computation.11.clone.1.clone.clone.clone.1 | loop fusion | flops 71303168 | bytes 8388608 | tf_op jit(solution)/shard_map/dot_general | solution.py:31
  74.7 0.0 copy-done.2
  74.7 0.0 copy-done.5
  74.7 0.2 broadcast_multiply_fusion
  74.9 0.0 copy-done
  74.9 1.4 multiply_convert_fusion.3
  76.4 12.6 %fusion.18 = bf16[1024,2048]{1,0:T(8,128)(2,1)} fusion(bf16[1024,2048]{1,0:T(8,128)(2,1)S(1)} %bitcast.61, bf16[2048,2048]{1,0:T(8,128)(2,1)} %multiply_convert_fusion.9), kind=kOutput, calls=%fused_computation.34 | convolution fusion | flops 8592031744 | bytes 16777216 | tf_op jit(solution)/shard_map/dot_general | solution.py:31
  89.0 11.1 %copy.24 = bf16[4,2,128,2048]{2,1,0,3:T(2,128)(2,1)} copy(bf16[4,2,128,2048]{3,2,1,0:T(8,128)(2,1)} %bitcast.62) | data formatting | bytes 8388608 | tf_op jit(solution)/shard_map/reshape | solution.py:32
  100.1 0.0 copy-start.3
  100.1 6.5 %all-to-all-start = ((bf16[4,2,128,2048]{2,1,0,3:T(2,128)(2,1)}), bf16[4,2,128,2048]{2,1,0,3:T(2,128)(2,1)}, u32[]{:S(2)}, u32[]{:S(2)}) async-start(bf16[4,2,128,2048]{2,1,0,3:T(2,128)(2,1)} %copy.24), calls=%async_computation | async-start | bytes 8388608 | tf_op jit(solution)/shard_map/all_to_all | solution.py:34
  106.6 0.0 copy-done.3
  106.6 75.3 %all-gather = s32[8,1,256]{2,1,0:T(1,128)S(1)} all-gather(s32[1,1,256]{2,1,0:T(1,128)S(1)} %bitcast.66), channel_id=1, replica_groups=mesh['member'=4,'slab'=8] {'slab'}, dimensions={0}, use_global_device_ids=true | all-gather | bytes 9216 | tf_op jit(solution)/shard_map/all_gather | solution.py:37
  181.9 0.1 reshape.231
  182.0 0.1 reshape.232
  182.1 0.1 add.140
  182.1 0.1 add.141
  182.3 18.5 %all-to-all-done = bf16[4,2,128,2048]{2,1,0,3:T(2,128)(2,1)} async-done(((bf16[4,2,128,2048]{2,1,0,3:T(2,128)(2,1)}), bf16[4,2,128,2048]{2,1,0,3:T(2,128)(2,1)}, u32[]{:S(2)}, u32[]{:S(2)}) %all-to-all-start) | async-done | bytes 4194336 | tf_op jit(solution)/shard_map/all_to_all | solution.py:34
  200.7 6.9 %copy.38 = bf16[4,2,128,8,256]{2,3,4,1,0:T(8,128)(2,1)} copy(bf16[4,2,128,8,256]{2,1,0,4,3:T(2,128)(2,1)} %bitcast.5) | data formatting | bytes 8388608 | tf_op jit(solution)/shard_map/all_to_all | solution.py:34
  207.6 7.3 %all_to_all.33 = bf16[4,2,1024,256]{2,3,1,0:T(8,128)(2,1)} reshape(bf16[4,2,8,128,256]{3,2,4,1,0:T(8,128)(2,1)} %bitcast.59) | data formatting | bytes 8388608 | tf_op jit(solution)/shard_map/all_to_all | solution.py:34
  214.9 23.3 %convert_bitcast_fusion.1 = bf16[4,2,1024,256]{2,3,1,0:T(8,128)(2,1)} fusion(bf16[4,2,1024,256]{2,3,1,0:T(8,128)(2,1)} %all_to_all.33), kind=kOutput, calls=%fused_computation.29 | convolution fusion | flops 4314890240 | bytes 8388608 | tf_op jit(solution)/shard_map/ya,mlac->mlyc/dot_general | solution.py:27
  238.2 6.2 %copy.26 = bf16[4,2,1024,256]{3,2,1,0:T(8,128)(2,1)} copy(bf16[4,2,1024,256]{2,3,1,0:T(8,128)(2,1)} %convert_bitcast_fusion.1) | data formatting | bytes 8388608 | tf_op jit(solution)/shard_map/convert_element_type | solution.py:28
  244.4 7.1 %reshape.236 = bf16[4,4096,128]{2,1,0:T(8,128)(2,1)} reshape(bf16[4,2,1024,256]{3,2,1,0:T(8,128)(2,1)} %copy.26) | data formatting | bytes 8388608 | tf_op jit(solution)/shard_map/reshape | solution.py:50
  251.5 7.6 %copy.27 = bf16[4,4096,128]{2,0,1:T(4,128)(2,1)} copy(bf16[4,4096,128]{2,1,0:T(8,128)(2,1)} %reshape.236) | data formatting | bytes 8388608 | tf_op jit(solution)/shard_map/reshape | solution.py:50
  259.1 3.8 gather_fusion.1
  262.9 6.0 %all-to-all-start.1 = ((bf16[4,256,128]{2,0,1:T(4,128)(2,1)}), bf16[4,256,128]{2,0,1:T(4,128)(2,1)S(1)}, u32[]{:S(2)}, u32[]{:S(2)}) async-start(bf16[4,256,128]{2,0,1:T(4,128)(2,1)} %bitcast.10), calls=%async_computation.1 | async-start | bytes 524288 | tf_op jit(solution)/shard_map/all_to_all | solution.py:51
  268.9 0.2 all-reduce.2.cloned.1.call-start
  269.1 7.4 %reshape.233 = bf16[4,4096,128]{2,1,0:T(8,128)(2,1)} reshape(bf16[4,2,128,2048]{3,2,1,0:T(8,128)(2,1)} %param.8) | data formatting | bytes 8388608 | tf_op jit(solution)/shard_map/reshape | solution.py:52
  276.5 0.0 copy-start.1
  276.5 0.0 copy-start.4
  276.5 7.6 %copy.23 = bf16[4,4096,128]{2,0,1:T(4,128)(2,1)} copy(bf16[4,4096,128]{2,1,0:T(8,128)(2,1)} %reshape.233) | data formatting | bytes 8388608 | tf_op jit(solution)/shard_map/reshape | solution.py:52
  284.1 3.2 gather_fusion
  287.3 0.0 all-to-all-done.1
  287.3 1.0 fusion.30
  288.4 0.0 all-reduce.2.cloned.1.call-update
  288.4 43.8 %all-reduce.2.cloned.1.call-done = f32[256,128]{1,0:T(8,128)} async-done(((f32[256,128]{1,0:T(8,128)}), f32[256,128]{1,0:T(8,128)}) %all-reduce.2.cloned.1.call-update) | async-done | bytes 131088 | tf_op jit(solution)/shard_map/psum | solution.py:54
  332.2 0.0 copy-done.1
  332.2 0.0 copy-done.4
  332.2 3.3 scatter_custom_fusion
  335.5 2.3 gather_fusion.2
  337.8 0.1 fusion.31
  337.9 14.1 %all_to_all.43 = bf16[4,256,128]{2,0,1:T(4,128)(2,1)S(1)} all-to-all(bf16[4,256,128]{2,0,1:T(4,128)(2,1)S(1)} %fusion.31), channel_id=1, replica_groups=mesh['member'=4,'slab'=8] {'slab'}, dimensions={1} | all-to-all | bytes 524288 | tf_op jit(solution)/shard_map/all_to_all | solution.py:60
  352.0 2.8 broadcast_in_dim.9
  354.9 28.1 %scatter_fusion = bf16[4,4096,128]{2,0,1:T(4,128)(2,1)} fusion(bf16[4,4096,128]{2,0,1:T(4,128)(2,1)} %broadcast_in_dim.9, s32[256]{0:T(256)S(1)} %bitcast.65, bf16[256,4,128]{2,1,0:T(4,128)(2,1)S(1)} %bitcast.63), kind=kCustom, calls=%fused_computation.4 | custom fusion | bytes 787456 | tf_op jit(solution)/shard_map/scatter | solution.py:62
  382.9 4.7 copy.28
  387.6 7.1 %reshape.237 = bf16[4,2,1024,256]{3,2,1,0:T(8,128)(2,1)} reshape(bf16[4,4096,128]{2,1,0:T(8,128)(2,1)} %copy.28) | data formatting | bytes 8388608 | tf_op jit(solution)/shard_map/reshape | solution.py:63
  394.7 23.8 %convert_bitcast_fusion = bf16[4,2,1024,256]{2,3,1,0:T(8,128)(2,1)} fusion(bf16[4,2,1024,256]{3,2,1,0:T(8,128)(2,1)} %reshape.237), kind=kOutput, calls=%fused_computation.28 | convolution fusion | flops 4314890240 | bytes 8388608 | tf_op jit(solution)/shard_map/ya,mlac->mlyc/dot_general | solution.py:27
  418.4 11.1 %copy.30 = bf16[4,2,1024,256]{3,1,0,2:T(2,128)(2,1)} copy(bf16[4,2,1024,256]{2,3,1,0:T(8,128)(2,1)} %convert_bitcast_fusion) | data formatting | bytes 8388608 | tf_op jit(solution)/shard_map/convert_element_type | solution.py:28
  429.6 4.8 all-to-all-start.3
  434.4 68.2 %fusion.75 = bf16[2048,2048,1,1]{1,0,3,2:T(8,128)(2,1)} fusion(), kind=kLoop, calls=%fused_computation.16.clone.clone.clone.1 | loop fusion | flops 71303168 | bytes 8388608 | tf_op jit(solution)/shard_map/dot_general | solution.py:65
  502.6 25.8 %all-to-all-done.3 = bf16[4,2,1024,256]{3,1,0,2:T(2,128)(2,1)} async-done(((bf16[4,2,1024,256]{3,1,0,2:T(2,128)(2,1)}), bf16[4,2,1024,256]{3,1,0,2:T(2,128)(2,1)}, u32[]{:S(2)}, u32[]{:S(2)}) %all-to-all-start.3) | async-done | bytes 4194336 | tf_op jit(solution)/shard_map/all_to_all | solution.py:64
  528.4 6.6 %copy.37 = bf16[4,2,8,128,256]{4,2,3,1,0:T(8,128)(2,1)} copy(bf16[4,2,8,128,256]{4,1,0,3,2:T(2,128)(2,1)} %bitcast.13) | data formatting | bytes 8388608 | tf_op jit(solution)/shard_map/all_to_all | solution.py:64
  534.9 7.4 %dot_general.17 = bf16[4,2,128,2048]{3,2,1,0:T(8,128)(2,1)} reshape(bf16[4,2,128,8,256]{4,3,2,1,0:T(8,128)(2,1)} %bitcast.60) | data formatting | bytes 8388608 | tf_op jit(solution)/shard_map/dot_general | solution.py:65
  542.3 14.5 %fusion.9 = f32[4,2,128,2048]{3,2,1,0:T(8,128)} fusion(bf16[4,2,128,2048]{3,2,1,0:T(8,128)(2,1)} %dot_general.17, f32[2,128,2048]{2,1,0:T(8,128)S(1)} %broadcast_multiply_fusion, bf16[2048,2048,1,1]{1,0,3,2:T(8,128)(2,1)} %fusion.75), kind=kOutput, calls=%fused_computation.22 | convolution fusion | flops 8592031744 | bytes 23068672 | tf_op jit(solution)/shard_map/dot_general | solution.py:65
  (7 shorter events, 0.1 us)
Async XLA Ops:
  6.5 68.2 %copy-start.2 = (f32[2,2048]{1,0:T(2,128)S(1)}, f32[2,2048]{1,0:T(2,128)}, u32[]{:S(2)}) copy-start(f32[2,2048]{1,0:T(2,128)} %param.10) | copy-start | bytes 49156
  6.5 68.2 %copy-start.5 = (f32[2,128]{1,0:T(2,128)S(1)}, f32[2,128]{1,0:T(2,128)}, u32[]{:S(2)}) copy-start(f32[2,128]{1,0:T(2,128)} %param.9) | copy-start | bytes 3076
  6.5 68.4 %copy-start = (f32[4,2,128,2048]{3,2,1,0:T(8,128)S(1)}, f32[4,2,128,2048]{3,2,1,0:T(8,128)}, u32[]{:S(2)}) copy-start(f32[4,2,128,2048]{3,2,1,0:T(8,128)} %param.7) | copy-start | bytes 25165828
  100.1 6.5 %copy-start.3 = (s32[256]{0:T(256)S(1)}, s32[256]{0:T(256)}, u32[]{:S(2)}) copy-start(s32[256]{0:T(256)} %param.11) | copy-start | bytes 3076
  100.1 100.6 %all-to-all-start = ((bf16[4,2,128,2048]{2,1,0,3:T(2,128)(2,1)}), bf16[4,2,128,2048]{2,1,0,3:T(2,128)(2,1)}, u32[]{:S(2)}, u32[]{:S(2)}) async-start(bf16[4,2,128,2048]{2,1,0,3:T(2,128)(2,1)} %copy.24), calls=%async_computation | async-start | bytes 8388608 | tf_op jit(solution)/shard_map/all_to_all | solution.py:34
  262.9 24.4 %all-to-all-start.1 = ((bf16[4,256,128]{2,0,1:T(4,128)(2,1)}), bf16[4,256,128]{2,0,1:T(4,128)(2,1)S(1)}, u32[]{:S(2)}, u32[]{:S(2)}) async-start(bf16[4,256,128]{2,0,1:T(4,128)(2,1)} %bitcast.10), calls=%async_computation.1 | async-start | bytes 524288 | tf_op jit(solution)/shard_map/all_to_all | solution.py:51
  268.9 63.3 %all-reduce.2.cloned.1.call-start = ((), (), s32[]{:S(2)}) async-start(), calls=%async_computation.4 | async-start | bytes 262144 | tf_op jit(solution)/shard_map/psum | solution.py:54
  276.5 55.7 %copy-start.1 = (f32[256,128]{1,0:T(8,128)S(1)}, f32[256,128]{1,0:T(8,128)}, u32[]{:S(2)}) copy-start(f32[256,128]{1,0:T(8,128)} %param.13) | copy-start | bytes 393220
  276.5 55.7 %copy-start.4 = (s32[256]{0:T(256)S(1)}, s32[256]{0:T(256)}, u32[]{:S(2)}) copy-start(s32[256]{0:T(256)} %param.12) | copy-start | bytes 3076
  429.6 98.8 %all-to-all-start.3 = ((bf16[4,2,1024,256]{3,1,0,2:T(2,128)(2,1)}), bf16[4,2,1024,256]{3,1,0,2:T(2,128)(2,1)}, u32[]{:S(2)}, u32[]{:S(2)}) async-start(bf16[4,2,1024,256]{3,1,0,2:T(2,128)(2,1)} %copy.30), calls=%async_computation.3 | async-start | bytes 8388608 | tf_op jit(solution)/shard_map/all_to_all | solution.py:64
Sparse Core Ops, SparseCore 0:
  288.5 43.6 all-reduce.1
where the time goes:
time: 572 us; the launch traced here: 564 us
  other arithmetic  142 us (25%)
  local copies, waits for them, and re-layouts  139 us (24%)
  blocking collectives  89.4 us (16%)
  waiting for transfers between devices  88.1 us (15%)
  matrix products  74.1 us (13%)
  starting transfers between devices  17.5 us (3%)
  between operations  13.7 us (2%)
    all_gather x1, blocking collectives, shards(): all_tiles = lax.all_gather(obs_tile, 'slab', axis=0, tiled=True)  75.3 us
    dot_general x1, other arithmetic, shards(): jnp.dot(back.reshape(-1, width), table_x, preferred_element_type=jnp.floa...  68.2 us
    dot_general x1, other arithmetic, shards(): jnp.dot(scaled.reshape(-1, width), table_x, preferred_element_type=jnp.fl...  68.2 us
    dot_general x2, matrix products, columns_pass(): jnp.einsum('ya,mlac->mlyc', table_y, block, preferred_element_type=jnp.fl...  47.1 us
    psum x1, waiting for transfers between devices, shards(): cells = lax.psum(partial_obs, 'member')  43.8 us
    scatter x2, local copies, waits for them, and re-layouts, shards(): filled = empty.at[:, flat_index].set(arrived)  32.7 us
    all_to_all x1, waiting for transfers between devices, shards(): lax.all_to_all(back_cols, 'slab', split_axis=2, concat_axis=3, tiled=True)  25.8 us
    all_to_all x1, waiting for transfers between devices, shards(): lax.all_to_all(along, 'slab', split_axis=3, concat_axis=2, tiled=True)  18.5 us
  transfers between devices with their start and end apart: 4, of which 3 were waited for; matrix products, arithmetic and copies ran while one was open for 15% of the time, Pallas kernels for 0%

commit v1 on v0

--- a/solution.py
+++ b/solution.py
@@ -51,7 +51,8 @@
     field_obs = lax.all_to_all(picked, "slab", split_axis=1, concat_axis=1, tiled=True)
     pert_obs = perturbation.reshape(members, -1, TILE)[:, obs_tile].astype(jnp.float32)
     partial_obs = jnp.sum(pert_obs * field_obs.astype(jnp.float32), axis=0)
-    cells = lax.psum(partial_obs, "member")
+    blocks = lax.all_gather(partial_obs, "member", axis=0, tiled=False)
+    cells = blocks.sum(axis=0)
     resid = cells - obs_value
     observed = jnp.arange(TILE, dtype=jnp.int32)[None, :] < obs_count[:, None]
     score = jnp.where(observed, resid / jnp.sqrt(1.0 + resid * resid / 4.0), 0.0)

time: 572 us -> 524 us (0.916)
  waiting for transfers between devices: 88.1 us -> 44.3 us
  between operations: 13.7 us -> 0.36 us
  blocking collectives: 89.4 us -> 99.9 us
    psum x1 -> x0, waiting for transfers between devices: 43.8 us -> none  [shards(): cells = lax.psum(partial_obs, 'member')]
    all_gather x0 -> x1, blocking collectives: none -> 10.6 us  [shards(): blocks = lax.all_gather(partial_obs, 'member', axis=0, tiled=False)]
  transfers between devices with their start and end apart: 4 -> 3, of which waited for: 3 -> 2; matrix products, arithmetic and copies ran while one was open for 15% -> 17% of each run, Pallas kernels for 0% -> 0%
where the time goes in v1:
time: 524 us; the launch traced here: 516 us
  other arithmetic  141 us (27%)
  local copies, waits for them, and re-layouts  139 us (27%)
  blocking collectives  99.9 us (19%)
  matrix products  74.1 us (14%)
  waiting for transfers between devices  44.3 us (8%)
  starting transfers between devices  17.5 us (3%)
    all_gather x1, blocking collectives, shards(): all_tiles = lax.all_gather(obs_tile, 'slab', axis=0, tiled=True)  75.3 us
    dot_general x1, other arithmetic, shards(): jnp.dot(back.reshape(-1, width), table_x, preferred_element_type=jnp.floa...  68.2 us
    dot_general x1, other arithmetic, shards(): jnp.dot(scaled.reshape(-1, width), table_x, preferred_element_type=jnp.fl...  68.2 us
    dot_general x2, matrix products, columns_pass(): jnp.einsum('ya,mlac->mlyc', table_y, block, preferred_element_type=jnp.fl...  47 us
    scatter x2, local copies, waits for them, and re-layouts, shards(): filled = empty.at[:, flat_index].set(arrived)  32.7 us
    all_to_all x1, waiting for transfers between devices, shards(): lax.all_to_all(back_cols, 'slab', split_axis=2, concat_axis=3, tiled=True)  25.8 us
    all_to_all x1, waiting for transfers between devices, shards(): lax.all_to_all(along, 'slab', split_axis=3, concat_axis=2, tiled=True)  18.5 us
    convert_element_type x2, local copies, waits for them, and re-layouts, columns_pass(): return product.astype(jnp.bfloat16)  17.3 us
  transfers between devices with their start and end apart: 3, of which 2 were waited for; matrix products, arithmetic and copies ran while one was open for 17% of the time, Pallas kernels for 0%

profile of v1, /device:TPU:0, one launch (start us, length us, event | category | flops | bytes accessed | tf_op | source)
XLA Modules:
  0.0 516.3 jit_solution(4024231199536054857)
XLA Ops:
  0.0 0.0 copy-start.2
  0.0 0.0 copy-start.5
  0.0 0.0 copy-start
  0.0 68.2 %multiply_convert_fusion.9 = bf16[2048,2048]{1,0:T(8,128)(2,1)} fusion(), kind=kLoop, calls=%fused_computation.11.clone.1.clone.clone.clone.1 | loop fusion | flops 71303168 | bytes 8388608 | tf_op jit(solution)/shard_map/dot_general | solution.py:31
  68.2 0.0 copy-done.2
  68.2 0.0 copy-done.5
  68.2 0.2 broadcast_multiply_fusion
  68.4 0.0 copy-done
  68.4 1.4 multiply_convert_fusion.3
  69.8 12.6 %fusion.18 = bf16[1024,2048]{1,0:T(8,128)(2,1)} fusion(bf16[1024,2048]{1,0:T(8,128)(2,1)S(1)} %bitcast.62, bf16[2048,2048]{1,0:T(8,128)(2,1)} %multiply_convert_fusion.9), kind=kOutput, calls=%fused_computation.34 | convolution fusion | flops 8592031744 | bytes 16777216 | tf_op jit(solution)/shard_map/dot_general | solution.py:31
  82.4 11.1 %copy.33 = bf16[4,2,128,2048]{2,1,0,3:T(2,128)(2,1)} copy(bf16[4,2,128,2048]{3,2,1,0:T(8,128)(2,1)} %bitcast.63) | data formatting | bytes 8388608 | tf_op jit(solution)/shard_map/reshape | solution.py:32
  93.6 0.0 copy-start.3
  93.6 6.5 %all-to-all-start = ((bf16[4,2,128,2048]{2,1,0,3:T(2,128)(2,1)}), bf16[4,2,128,2048]{2,1,0,3:T(2,128)(2,1)}, u32[]{:S(2)}, u32[]{:S(2)}) async-start(bf16[4,2,128,2048]{2,1,0,3:T(2,128)(2,1)} %copy.33), calls=%async_computation | async-start | bytes 8388608 | tf_op jit(solution)/shard_map/all_to_all | solution.py:34
  100.1 0.0 copy-done.3
  100.1 75.3 %all-gather.1 = s32[8,1,256]{2,1,0:T(1,128)S(1)} all-gather(s32[1,1,256]{2,1,0:T(1,128)S(1)} %bitcast.68), channel_id=1, replica_groups=mesh['member'=4,'slab'=8] {'slab'}, dimensions={0}, use_global_device_ids=true | all-gather | bytes 9216 | tf_op jit(solution)/shard_map/all_gather | solution.py:37
  175.4 0.1 reshape.231
  175.5 0.1 reshape.232
  175.5 0.1 add.138
  175.6 0.1 add.139
  175.7 18.5 %all-to-all-done = bf16[4,2,128,2048]{2,1,0,3:T(2,128)(2,1)} async-done(((bf16[4,2,128,2048]{2,1,0,3:T(2,128)(2,1)}), bf16[4,2,128,2048]{2,1,0,3:T(2,128)(2,1)}, u32[]{:S(2)}, u32[]{:S(2)}) %all-to-all-start) | async-done | bytes 4194336 | tf_op jit(solution)/shard_map/all_to_all | solution.py:34
  194.2 6.9 %copy.47 = bf16[4,2,128,8,256]{2,3,4,1,0:T(8,128)(2,1)} copy(bf16[4,2,128,8,256]{2,1,0,4,3:T(2,128)(2,1)} %bitcast.5) | data formatting | bytes 8388608 | tf_op jit(solution)/shard_map/all_to_all | solution.py:34
  201.1 7.3 %all_to_all.33 = bf16[4,2,1024,256]{2,3,1,0:T(8,128)(2,1)} reshape(bf16[4,2,8,128,256]{3,2,4,1,0:T(8,128)(2,1)} %bitcast.60) | data formatting | bytes 8388608 | tf_op jit(solution)/shard_map/all_to_all | solution.py:34
  208.4 23.3 %convert_bitcast_fusion.1 = bf16[4,2,1024,256]{2,3,1,0:T(8,128)(2,1)} fusion(bf16[4,2,1024,256]{2,3,1,0:T(8,128)(2,1)} %all_to_all.33), kind=kOutput, calls=%fused_computation.29 | convolution fusion | flops 4314890240 | bytes 8388608 | tf_op jit(solution)/shard_map/ya,mlac->mlyc/dot_general | solution.py:27
  231.7 6.2 %copy.35 = bf16[4,2,1024,256]{3,2,1,0:T(8,128)(2,1)} copy(bf16[4,2,1024,256]{2,3,1,0:T(8,128)(2,1)} %convert_bitcast_fusion.1) | data formatting | bytes 8388608 | tf_op jit(solution)/shard_map/convert_element_type | solution.py:28
  237.9 7.1 %reshape.236 = bf16[4,4096,128]{2,1,0:T(8,128)(2,1)} reshape(bf16[4,2,1024,256]{3,2,1,0:T(8,128)(2,1)} %copy.35) | data formatting | bytes 8388608 | tf_op jit(solution)/shard_map/reshape | solution.py:50
  245.0 7.6 %copy.36 = bf16[4,4096,128]{2,0,1:T(4,128)(2,1)} copy(bf16[4,4096,128]{2,1,0:T(8,128)(2,1)} %reshape.236) | data formatting | bytes 8388608 | tf_op jit(solution)/shard_map/reshape | solution.py:50
  252.5 3.8 gather_fusion.1
  256.4 6.2 %all-to-all-start.1 = ((bf16[4,256,128]{2,0,1:T(4,128)(2,1)}), bf16[4,256,128]{2,0,1:T(4,128)(2,1)S(1)}, u32[]{:S(2)}, u32[]{:S(2)}) async-start(bf16[4,256,128]{2,0,1:T(4,128)(2,1)} %bitcast.10), calls=%async_computation.1 | async-start | bytes 524288 | tf_op jit(solution)/shard_map/all_to_all | solution.py:51
  262.6 7.4 %reshape.233 = bf16[4,4096,128]{2,1,0:T(8,128)(2,1)} reshape(bf16[4,2,128,2048]{3,2,1,0:T(8,128)(2,1)} %param.8) | data formatting | bytes 8388608 | tf_op jit(solution)/shard_map/reshape | solution.py:52
  270.0 0.0 copy-start.1
  270.0 0.0 copy-start.4
  270.0 7.6 %copy.32 = bf16[4,4096,128]{2,0,1:T(4,128)(2,1)} copy(bf16[4,4096,128]{2,1,0:T(8,128)(2,1)} %reshape.233) | data formatting | bytes 8388608 | tf_op jit(solution)/shard_map/reshape | solution.py:52
  277.6 3.2 gather_fusion
  280.8 0.0 all-to-all-done.1
  280.8 0.4 fusion.30
  281.2 10.6 %all-gather = f32[1024,128]{1,0:T(8,128)S(1)} all-gather(f32[256,128]{1,0:T(8,128)S(1)} %fusion.30), channel_id=2, replica_groups=mesh['member'=4,'slab'=8] {'member'}, dimensions={0}, use_global_device_ids=true | all-gather | bytes 655360 | tf_op jit(solution)/shard_map/all_gather | solution.py:54
  291.9 0.0 copy-done.1
  291.9 0.0 copy-done.4
  291.9 2.9 scatter_custom_fusion
  294.8 2.3 gather_fusion.2
  297.1 0.1 fusion.31
  297.2 14.0 %all_to_all.43 = bf16[4,256,128]{2,0,1:T(4,128)(2,1)S(1)} all-to-all(bf16[4,256,128]{2,0,1:T(4,128)(2,1)S(1)} %fusion.31), channel_id=1, replica_groups=mesh['member'=4,'slab'=8] {'slab'}, dimensions={1} | all-to-all | bytes 524288 | tf_op jit(solution)/shard_map/all_to_all | solution.py:61
  311.3 2.8 broadcast_in_dim.9
  314.1 28.1 %scatter_fusion = bf16[4,4096,128]{2,0,1:T(4,128)(2,1)} fusion(bf16[4,4096,128]{2,0,1:T(4,128)(2,1)} %broadcast_in_dim.9, s32[256]{0:T(256)S(1)} %bitcast.67, bf16[256,4,128]{2,1,0:T(4,128)(2,1)S(1)} %bitcast.65), kind=kCustom, calls=%fused_computation.4 | custom fusion | bytes 787456 | tf_op jit(solution)/shard_map/scatter | solution.py:63
  342.1 4.7 copy.37
  346.8 7.1 %reshape.237 = bf16[4,2,1024,256]{3,2,1,0:T(8,128)(2,1)} reshape(bf16[4,4096,128]{2,1,0:T(8,128)(2,1)} %copy.37) | data formatting | bytes 8388608 | tf_op jit(solution)/shard_map/reshape | solution.py:64
  353.9 23.8 %convert_bitcast_fusion = bf16[4,2,1024,256]{2,3,1,0:T(8,128)(2,1)} fusion(bf16[4,2,1024,256]{3,2,1,0:T(8,128)(2,1)} %reshape.237), kind=kOutput, calls=%fused_computation.28 | convolution fusion | flops 4314890240 | bytes 8388608 | tf_op jit(solution)/shard_map/ya,mlac->mlyc/dot_general | solution.py:27
  377.6 11.1 %copy.39 = bf16[4,2,1024,256]{3,1,0,2:T(2,128)(2,1)} copy(bf16[4,2,1024,256]{2,3,1,0:T(8,128)(2,1)} %convert_bitcast_fusion) | data formatting | bytes 8388608 | tf_op jit(solution)/shard_map/convert_element_type | solution.py:28
  388.8 4.8 all-to-all-start.3
  393.6 68.2 %fusion.75 = bf16[2048,2048,1,1]{1,0,3,2:T(8,128)(2,1)} fusion(), kind=kLoop, calls=%fused_computation.16.clone.clone.clone.1 | loop fusion | flops 71303168 | bytes 8388608 | tf_op jit(solution)/shard_map/dot_general | solution.py:66
  461.8 25.8 %all-to-all-done.3 = bf16[4,2,1024,256]{3,1,0,2:T(2,128)(2,1)} async-done(((bf16[4,2,1024,256]{3,1,0,2:T(2,128)(2,1)}), bf16[4,2,1024,256]{3,1,0,2:T(2,128)(2,1)}, u32[]{:S(2)}, u32[]{:S(2)}) %all-to-all-start.3) | async-done | bytes 4194336 | tf_op jit(solution)/shard_map/all_to_all | solution.py:65
  487.6 6.6 %copy.46 = bf16[4,2,8,128,256]{4,2,3,1,0:T(8,128)(2,1)} copy(bf16[4,2,8,128,256]{4,1,0,3,2:T(2,128)(2,1)} %bitcast.14) | data formatting | bytes 8388608 | tf_op jit(solution)/shard_map/all_to_all | solution.py:65
  494.1 7.4 %dot_general.17 = bf16[4,2,128,2048]{3,2,1,0:T(8,128)(2,1)} reshape(bf16[4,2,128,8,256]{4,3,2,1,0:T(8,128)(2,1)} %bitcast.61) | data formatting | bytes 8388608 | tf_op jit(solution)/shard_map/dot_general | solution.py:66
  501.6 14.5 %fusion.9 = f32[4,2,128,2048]{3,2,1,0:T(8,128)} fusion(bf16[4,2,128,2048]{3,2,1,0:T(8,128)(2,1)} %dot_general.17, f32[2,128,2048]{2,1,0:T(8,128)S(1)} %broadcast_multiply_fusion, bf16[2048,2048,1,1]{1,0,3,2:T(8,128)(2,1)} %fusion.75), kind=kOutput, calls=%fused_computation.22 | convolution fusion | flops 8592031744 | bytes 23068672 | tf_op jit(solution)/shard_map/dot_general | solution.py:66
  (8 shorter events, 0.1 us)
Async XLA Ops:
  0.0 68.2 %copy-start.2 = (f32[2,2048]{1,0:T(2,128)S(1)}, f32[2,2048]{1,0:T(2,128)}, u32[]{:S(2)}) copy-start(f32[2,2048]{1,0:T(2,128)} %param.10) | copy-start | bytes 49156
  0.0 68.2 %copy-start.5 = (f32[2,128]{1,0:T(2,128)S(1)}, f32[2,128]{1,0:T(2,128)}, u32[]{:S(2)}) copy-start(f32[2,128]{1,0:T(2,128)} %param.9) | copy-start | bytes 3076
  0.0 68.4 %copy-start = (f32[4,2,128,2048]{3,2,1,0:T(8,128)S(1)}, f32[4,2,128,2048]{3,2,1,0:T(8,128)}, u32[]{:S(2)}) copy-start(f32[4,2,128,2048]{3,2,1,0:T(8,128)} %param.7) | copy-start | bytes 25165828
  93.6 6.5 %copy-start.3 = (s32[256]{0:T(256)S(1)}, s32[256]{0:T(256)}, u32[]{:S(2)}) copy-start(s32[256]{0:T(256)} %param.11) | copy-start | bytes 3076
  93.6 100.6 %all-to-all-start = ((bf16[4,2,128,2048]{2,1,0,3:T(2,128)(2,1)}), bf16[4,2,128,2048]{2,1,0,3:T(2,128)(2,1)}, u32[]{:S(2)}, u32[]{:S(2)}) async-start(bf16[4,2,128,2048]{2,1,0,3:T(2,128)(2,1)} %copy.33), calls=%async_computation | async-start | bytes 8388608 | tf_op jit(solution)/shard_map/all_to_all | solution.py:34
  256.4 24.4 %all-to-all-start.1 = ((bf16[4,256,128]{2,0,1:T(4,128)(2,1)}), bf16[4,256,128]{2,0,1:T(4,128)(2,1)S(1)}, u32[]{:S(2)}, u32[]{:S(2)}) async-start(bf16[4,256,128]{2,0,1:T(4,128)(2,1)} %bitcast.10), calls=%async_computation.1 | async-start | bytes 524288 | tf_op jit(solution)/shard_map/all_to_all | solution.py:51
  270.0 21.9 %copy-start.1 = (f32[256,128]{1,0:T(8,128)S(1)}, f32[256,128]{1,0:T(8,128)}, u32[]{:S(2)}) copy-start(f32[256,128]{1,0:T(8,128)} %param.13) | copy-start | bytes 393220
  270.0 21.9 %copy-start.4 = (s32[256]{0:T(256)S(1)}, s32[256]{0:T(256)}, u32[]{:S(2)}) copy-start(s32[256]{0:T(256)} %param.12) | copy-start | bytes 3076
  388.8 98.8 %all-to-all-start.3 = ((bf16[4,2,1024,256]{3,1,0,2:T(2,128)(2,1)}), bf16[4,2,1024,256]{3,1,0,2:T(2,128)(2,1)}, u32[]{:S(2)}, u32[]{:S(2)}) async-start(bf16[4,2,1024,256]{3,1,0,2:T(2,128)(2,1)} %copy.39), calls=%async_computation.3 | async-start | bytes 8388608 | tf_op jit(solution)/shard_map/all_to_all | solution.py:65
